TPU v7x, 32 devices: a whole 2x2x4 slice. The times are simulated.
32 devices in a mesh: seq: 8 (over z, y), head: 4 (over x, core).
Axes of the slice: x: 2, y: 2, z: 4, core: 2. Of those that a mesh axis runs over, the one named last changes fastest.
Arguments:
- queries: bfloat16 [1024, 3584], P('seq', 'head'), may hold values from -256 to 256
- key_codes: bfloat16 [1024, 512], P('seq', 'head'), may hold values from -4 to 4
- value_codes: bfloat16 [1024, 512], P('seq', 'head'), may hold values from -4 to 4
- kv_scales: float32 [2, 8, 4], P(None, 'seq', 'head'), may hold values from 0.5 to 2
- out_weight: bfloat16 [3584, 3584], P('head'), may hold values from -0.09375 to 0.09375
- turn_ids: int32 [1024], replicated, may hold values from 0 to 7, never falling along the last dimension, each value on 1 to 256 neighbouring positions
- block_mask: int32 [8, 8], P('seq'), may hold values 0 or 1
- doc_lengths: int32 [4], replicated, may hold values from 1 to 512, 1024 in all
Outputs:
- projected: bfloat16 [1024, 3584], P('seq', 'head')
All inputs are finite; a program needn't handle non-finite values. No bound on the sum of `block_mask` on one device may be relied on, other than what follows from the above.
Results may differ from a plain program's by a relative error of at most 0.012.
Values may be sent and summed in bfloat16 or wider, within the bound.
No kernel may reach another device: no remote copies, remote signals or barrier semaphores. Data moves between devices by JAX's collectives and lax.ppermute only.
A program may use at most 128 MiB of HBM per device.

v0:
```python
import math
import jax
import jax.numpy as jnp
from jax import lax
from jax.sharding import PartitionSpec as P

HEAD_DIM = 128
BLOCK = 128
masked_score = -1e30


def document_of(places, doc_lengths):
    ends = jnp.cumsum(doc_lengths)
    return jnp.sum((places[:, None] >= ends[None, :]).astype(jnp.int32), axis=1)


def dequantize(codes, scales):
    blocks = scales.shape[0]
    shaped = codes.astype(jnp.float32).reshape(blocks, -1, codes.shape[1])
    return (shaped * scales[:, None, None]).reshape(codes.shape).astype(jnp.bfloat16)


def on_device(
    queries, key_codes, value_codes, kv_scales, out_weight, turn_ids, block_mask, doc_lengths
):
    row_count = queries.shape[0]
    groups = queries.shape[1] // HEAD_DIM
    mine = lax.axis_index("seq")
    scaling = 1.0 / math.sqrt(HEAD_DIM)
    keys = dequantize(key_codes, kv_scales[0, :, 0])
    values = dequantize(value_codes, kv_scales[1, :, 0])
    key_value = jnp.stack([keys, values])
    query_heads = queries.reshape(row_count, groups, HEAD_DIM)
    offsets = jnp.arange(row_count, dtype=jnp.int32)
    query_places = mine * row_count + offsets
    query_turns = lax.dynamic_slice_in_dim(turn_ids, mine * row_count, row_count)
    query_docs = document_of(query_places, doc_lengths)
    mask_rows = block_mask[offsets // BLOCK]
    pair = lax.all_gather(key_value, "seq", axis=1, tiled=True)
    width = pair.shape[1]
    key_places = jnp.arange(width, dtype=jnp.int32)
    key_docs = document_of(key_places, doc_lengths)
    kept = jnp.take(mask_rows, key_places // BLOCK, axis=1) > 0
    same_block = (query_places // BLOCK)[:, None] == (key_places // BLOCK)[None, :]
    allowed = (
        (key_places[None, :] <= query_places[:, None])
        & (query_docs[:, None] == key_docs[None, :])
        & ((query_turns[:, None] == turn_ids[None, :]) | kept | same_block)
    )
    best = jnp.full((groups, row_count), masked_score, jnp.float32)
    scores = (
        jnp.einsum("qgd,kd->gqk", query_heads, pair[0], preferred_element_type=jnp.float32)
        * scaling
    )
    scores = jnp.where(allowed[None], scores, masked_score)
    newest = jnp.maximum(best, jnp.max(scores, axis=2))
    weights = jnp.where(allowed[None], jnp.exp(scores - newest[:, :, None]), 0.0)
    totals = jnp.sum(weights, axis=2)
    summed = jnp.einsum(
        "gqk,kd->gqd", weights.astype(jnp.bfloat16), pair[1], preferred_element_type=jnp.float32
    )
    state = (newest, totals, summed)
    best, totals, summed = state
    attended = (summed / totals[:, :, None]).astype(jnp.bfloat16)
    weight_heads = out_weight.reshape(groups, HEAD_DIM, out_weight.shape[1])
    partial_value = jnp.einsum(
        "gqd,gde->qe", attended, weight_heads, preferred_element_type=jnp.float32
    )
    return lax.psum_scatter(
        partial_value.astype(jnp.bfloat16), "head", scatter_dimension=1, tiled=True
    )


def solution(mesh):
    placed = (
        P("seq", "head"),
        P("seq", "head"),
        P("seq", "head"),
        P(None, "seq", "head"),
        P("head", None),
        P(),
        P("seq", None),
        P(),
    )
    return jax.shard_map(
        on_device, mesh=mesh, in_specs=placed, out_specs=P("seq", "head"), check_vma=False
    )
```

profile of v0, /device:TPU:0, one launch (start us, length us, event | category | flops | bytes accessed | tf_op | source)
XLA Modules:
  0.0 95.0 jit_solution(5045930761843892157)
XLA Ops:
  6.5 0.0 copy-start
  6.5 0.0 copy-start.2
  6.5 0.0 reduce-scatter.4.cloned.1.call-start
  6.6 0.8 reduce-window.8
  7.4 0.1 convert_reduce_fusion
  7.5 0.1 convert_reduce_fusion.1
  7.6 1.4 %fusion.33 = (f32[1,1,1]{0,2,1:T(1,128)}, f32[1,1,1]{0,2,1:T(1,128)}) fusion(f32[2,1,1]{0,2,1:T(1,128)} %param.11), kind=kLoop, calls=%fused_computation.55 | loop fusion | bytes 16 | tf_op jit(solution)/shard_map/slice | solution.py:30
  9.0 1.1 %copy.15 = bf16[128,896]{0,1:T(8,128)(2,1)S(1)} copy(bf16[128,896]{1,0:T(8,128)(2,1)} %param.8) | data formatting | bytes 458752 | tf_op args[0]
  10.1 2.1 %fusion.22 = (bf16[1,128,128]{2,1,0:T(8,128)(2,1)S(1)}, bf16[1,128,128]{2,1,0:T(8,128)(2,1)S(1)}) fusion(bf16[128,128]{1,0:T(8,128)(2,1)} %param.9, f32[]{:T(128)} %bitcast.5, f32[]{:T(128)} %bitcast.7, bf16[128,128]{1,0:T(8,128)(2,1)} %param.10), kind=kLoop, calls=%fused_computation.26 | loop fusion | flops 98304 | bytes 131080 | tf_op jit(solution)/shard_map/convert_element_type | solution.py:20
  12.2 33.0 %all_gather.3 = bf16[2,1024,128]{2,1,0:T(8,128)(2,1)S(1)} all-gather(bf16[2,128,128]{2,1,0:T(8,128)(2,1)S(1)} %pad_maximum_fusion), channel_id=1, replica_groups=mesh['seq'=8,'head'=4] {'seq'}, dimensions={1}, use_global_device_ids=true | all-gather | bytes 589824 | tf_op jit(solution)/shard_map/all_gather | solution.py:39
  45.3 0.8 dynamic_slice.3
  46.0 0.0 copy-done
  46.0 0.1 broadcast.312
  46.1 2.8 %gather_fusion = s32[1024,128]{1,0:T(8,128)S(1)} fusion(s32[128,8]{0,1:T(8,128)S(1)} %broadcast.312, s32[1024]{0:T(1024)S(1)} %broadcast_clamp_fusion), kind=kCustom, calls=%fused_computation | custom fusion | bytes 1052672 | tf_op jit(solution)/shard_map/jit(_take)/gather | solution.py:43
  48.9 0.0 copy-done.2
  48.9 1.0 %fusion.16 = pred[128,1024]{0,1:T(8,128)(4,1)S(1)} fusion(s32[1024,128]{1,0:T(8,128)S(1)} %gather_fusion, s32[128]{0:T(128)S(1)} %get-tuple-element.9, s32[128]{0:T(128)S(1)} %dynamic_slice.3, s32[128]{0:T(128)S(1)} %convert_reduce_fusion.1, s32[128]{0:T(128)S(1)} %get-tuple-element.10, s32[1024]{0:T(1024)S(1)} %add_select_fusion, s32[1024]{0:T(1024)S(1)} %copy-done.2, ...), kind=kLoop, calls=%fused_computation.15 | loop fusion | flops 1310720 | bytes 670720 | tf_op jit(solution)/shard_map/and | solution.py:46
  50.0 0.7 fusion.1
  50.6 0.0 copy-start.1
  50.7 1.8 %copy-done.1 = f32[1024,128,7]{1,0,2:T(8,128)} copy-done((f32[1024,128,7]{1,0,2:T(8,128)}, f32[1024,128,7]{1,0,2:T(8,128)S(1)}, u32[]{:S(2)}) %copy-start.1) | copy-done | bytes 3670040
  52.4 0.9 fusion.2
  53.3 6.5 %fusion = bf16[128,3584]{1,0:T(8,128)(2,1)S(1)} fusion(bf16[7,128,3584]{2,1,0:T(8,128)(2,1)} %bitcast.63, f32[1024,128,7]{1,0,2:T(8,128)} %copy-done.1, f32[7,128]{1,0:T(8,128)S(1)} %broadcast_maximum_fusion, pred[128,1024]{0,1:T(8,128)(4,1)S(1)} %fusion.16, bf16[2,1024,128]{2,1,0:T(8,128)(2,1)S(1)} %all_gather.3, f32[7,128]{1,0:T(8,128)S(1)} %fusion.2), kind=kOutput, calls=%fused_computation.2 | convolution fusion | flops 1062240256 | bytes 11411456 | tf_op jit(solution)/shard_map/gqd,gde->qe/dot_general | solution.py:66
  59.8 1.3 %copy.20 = bf16[128,3584]{0,1:T(8,128)(2,1)} copy(bf16[128,3584]{1,0:T(8,128)(2,1)S(1)} %fusion) | data formatting | bytes 1835008
  61.1 0.0 reduce-scatter.4.cloned.1.call-update
  61.1 25.2 %reduce-scatter.4.cloned.1.call-done = bf16[896,128]{1,0:T(8,128)(2,1)} async-done(((bf16[3584,128]{1,0:T(8,128)(2,1)}), bf16[896,128]{1,0:T(8,128)(2,1)}) %reduce-scatter.4.cloned.1.call-update) | async-done | bytes 229392
  86.4 1.8 %copy.21 = bf16[128,896]{1,0:T(8,128)(2,1)} copy(bf16[128,896]{0,1:T(8,128)(2,1)} %bitcast.59) | data formatting | bytes 458752
  (7 shorter events, 0.0 us)
Async XLA Ops:
  6.5 39.5 %copy-start = (s32[1,8]{1,0:T(1,128)S(1)}, s32[1,8]{1,0:T(1,128)}, u32[]{:S(2)}) copy-start(s32[1,8]{1,0:T(1,128)} %param.14) | copy-start | bytes 100
  6.5 42.4 %copy-start.2 = (s32[1024]{0:T(1024)S(1)}, s32[1024]{0:T(1024)}, u32[]{:S(2)}) copy-start(s32[1024]{0:T(1024)} %param.13) | copy-start | bytes 12292
  6.5 79.8 %reduce-scatter.4.cloned.1.call-start = ((), (), s32[]{:S(2)}) async-start(), calls=%async_computation.1 | async-start | bytes 1146880
  50.6 1.8 %copy-start.1 = (f32[1024,128,7]{1,0,2:T(8,128)}, f32[1024,128,7]{1,0,2:T(8,128)S(1)}, u32[]{:S(2)}) copy-start(f32[1024,128,7]{1,0,2:T(8,128)S(1)} %get-tuple-element.8) | copy-start | bytes 11010052
Sparse Core Ops, SparseCore 0:
  61.2 25.0 reduce-scatter.3
where the time goes:
time: 95.3 us; the launch traced here: 95 us
  blocking collectives  33 us (35%)
  waiting for transfers between devices  25.3 us (27%)
  between operations  13.5 us (14%)
  local copies, waits for them, and re-layouts  11 us (12%)
  matrix products  7.15 us (8%)
  other arithmetic  5.07 us (5%)
    all_gather x1, blocking collectives, on_device(): pair = lax.all_gather(key_value, 'seq', axis=1, tiled=True)  33 us
    unnamed x2, waiting for transfers between devices  25.3 us
    dot_general x1, matrix products, on_device(): jnp.einsum('gqd,gde->qe', attended, weight_heads, preferred_element_type=...  6.46 us
    unnamed x9, local copies, waits for them, and re-layouts  5.94 us
    gather x1, local copies, waits for them, and re-layouts, on_device(): kept = jnp.take(mask_rows, key_places // BLOCK, axis=1) > 0  2.81 us
    convert_element_type x1, other arithmetic, dequantize(): (shaped * scales[:, None, None]).reshape(codes.shape).astype(jnp.bfloat16)  2.13 us
  transfers between devices with their start and end apart: 1, of which 1 were waited for; matrix products, arithmetic and copies ran while one was open for 0% of the time, Pallas kernels for 0%

commit v1 on v0

--- a/solution.py
+++ b/solution.py
@@ -7,6 +7,33 @@
 HEAD_DIM = 128
 BLOCK = 128
 masked_score = -1e30
+
+
+def layers_all_review(chunk, d0):
+    right_arr = list(chunk.shape[1:])
+    right_arr[d0] *= chunk.shape[0]
+    local_out = jnp.moveaxis(chunk, 0, d0).reshape(right_arr)
+    return local_out
+
+
+def _treat_corner(q_in, chip_axis):
+    found_now = lax.axis_index(chip_axis)
+    a_next = lax.axis_size(chip_axis)
+    raw_out, state_now = (a_next, found_now)
+    f_now, z_new = (q_in[None], 1)
+    while z_new < raw_out:
+        v1 = lax.ppermute(f_now, chip_axis, [(p, p ^ z_new) for p in range(raw_out)])
+        tmp = state_now & z_new == 0
+        w1 = jnp.where(tmp, f_now, v1)
+        f_now = jnp.concatenate([w1, jnp.where(tmp, v1, f_now)])
+        z_new *= 2
+    return f_now
+
+
+def inputs_arrange(panel, xin, join_dim=1):
+    carry = _treat_corner(panel, xin)
+    earlier = layers_all_review(carry, join_dim)
+    return earlier
 
 
 def document_of(places, doc_lengths):
@@ -36,7 +63,7 @@
     query_turns = lax.dynamic_slice_in_dim(turn_ids, mine * row_count, row_count)
     query_docs = document_of(query_places, doc_lengths)
     mask_rows = block_mask[offsets // BLOCK]
-    pair = lax.all_gather(key_value, "seq", axis=1, tiled=True)
+    pair = inputs_arrange(key_value, "seq")
     width = pair.shape[1]
     key_places = jnp.arange(width, dtype=jnp.int32)
     key_docs = document_of(key_places, doc_lengths)

time: 95.3 us -> 78.9 us (0.83)
  blocking collectives: 33 us -> 0 us
  starting transfers between devices: 0.01 us -> 8.3 us
  waiting for transfers between devices: 25.3 us -> 33.3 us
    all_gather x1 -> x0, blocking collectives: 33 us -> none  [on_device(): pair = lax.all_gather(key_value, 'seq', axis=1, tiled=True)]
    ppermute x0 -> x3, starting transfers between devices: none -> 8.3 us  [_treat_corner(): lax.ppermute(f_now, chip_axis, [(p, p ^ z_new) for p in range(raw_out)])]
    ppermute x0 -> x3, waiting for transfers between devices: none -> 7.98 us  [_treat_corner(): lax.ppermute(f_now, chip_axis, [(p, p ^ z_new) for p in range(raw_out)])]
  transfers between devices with their start and end apart: 1 -> 4, of which waited for: 1 -> 4; matrix products, arithmetic and copies ran while one was open for 0% -> 9% of each run, Pallas kernels for 0% -> 0%
where the time goes in v1:
time: 78.9 us; the launch traced here: 78.6 us
  waiting for transfers between devices  33.3 us (42%)
  between operations  13.5 us (17%)
  local copies, waits for them, and re-layouts  11 us (14%)
  starting transfers between devices  8.3 us (11%)
  matrix products  7.16 us (9%)
  other arithmetic  5.24 us (7%)
    unnamed x2, waiting for transfers between devices  25.4 us
    ppermute x3, starting transfers between devices, _treat_corner(): lax.ppermute(f_now, chip_axis, [(p, p ^ z_new) for p in range(raw_out)])  8.3 us
    ppermute x3, waiting for transfers between devices, _treat_corner(): lax.ppermute(f_now, chip_axis, [(p, p ^ z_new) for p in range(raw_out)])  7.98 us
    dot_general x1, matrix products, on_device(): jnp.einsum('gqd,gde->qe', attended, weight_heads, preferred_element_type=...  6.47 us
    unnamed x9, local copies, waits for them, and re-layouts  5.94 us
    gather x1, local copies, waits for them, and re-layouts, on_device(): kept = jnp.take(mask_rows, key_places // BLOCK, axis=1) > 0  2.81 us
    convert_element_type x1, other arithmetic, dequantize(): (shaped * scales[:, None, None]).reshape(codes.shape).astype(jnp.bfloat16)  2.12 us
  transfers between devices with their start and end apart: 4, of which 4 were waited for; matrix products, arithmetic and copies ran while one was open for 9% of the time, Pallas kernels for 0%

profile of v1, /device:TPU:0, one launch (start us, length us, event | category | flops | bytes accessed | tf_op | source)
XLA Modules:
  0.0 78.6 jit_solution(617980751805996241)
XLA Ops:
  6.5 0.0 copy-start
  6.5 0.0 copy-start.2
  6.5 0.0 reduce-scatter.4.cloned.1.call-start
  6.5 1.4 %fusion.33 = (f32[1,1,1]{0,2,1:T(1,128)}, f32[1,1,1]{0,2,1:T(1,128)}) fusion(f32[2,1,1]{0,2,1:T(1,128)} %param.11), kind=kLoop, calls=%fused_computation.62 | loop fusion | bytes 16 | tf_op jit(solution)/shard_map/slice | solution.py:57
  7.9 2.1 %fusion.21 = (bf16[1,128,128]{2,1,0:T(8,128)(2,1)S(1)}, bf16[1,128,128]{2,1,0:T(8,128)(2,1)S(1)}) fusion(bf16[128,128]{1,0:T(8,128)(2,1)} %param.9, f32[]{:T(128)} %bitcast.5, f32[]{:T(128)} %bitcast.7, bf16[128,128]{1,0:T(8,128)(2,1)} %param.10), kind=kLoop, calls=%fused_computation.32 | loop fusion | flops 98304 | bytes 131080 | tf_op jit(solution)/shard_map/convert_element_type | solution.py:47
  10.1 3.1 %collective-permute-start = (bf16[1,2,128,128]{3,2,1,0:T(8,128)(2,1)S(1)}, bf16[1,2,128,128]{3,2,1,0:T(8,128)(2,1)S(1)}, u32[]{:S(2)}, u32[]{:S(2)}) collective-permute-start(bf16[1,2,128,128]{3,2,1,0:T(8,128)(2,1)S(1)} %maximum_bitcast_fusion.1), channel_id=1, source_target_pairs={{0,4},{4,0},{8,12},{12,8},{16,20},{20,16},{24,28},{28,24},{1,5},{5... | collective-permute-start | bytes 196616 | tf_op jit(solution)/shard_map/ppermute | solution.py:25
  13.1 0.8 %reduce-window.8 = s32[4,1]{0,1:T(1,128)S(1)} reduce-window(s32[4,1]{0,1:T(1,128)} %bitcast.71, s32[]{:T(128)} %constant.73.clone.1), window={size=4x1 pad=3_0x0_0}, to_apply=%region_0.0 | reduce-window | flops 12 | bytes 36 | tf_op jit(solution)/shard_map/reduce-window.3
  14.0 0.1 convert_reduce_fusion
  14.1 1.3 %collective-permute-done = bf16[1,2,128,128]{3,2,1,0:T(8,128)(2,1)S(1)} collective-permute-done((bf16[1,2,128,128]{3,2,1,0:T(8,128)(2,1)S(1)}, bf16[1,2,128,128]{3,2,1,0:T(8,128)(2,1)S(1)}, u32[]{:S(2)}, u32[]{:S(2)}) %collective-permute-start) | collective-permute-done | bytes 65568 | tf_op jit(solution)/shard_map/ppermute | solution.py:25
  15.4 2.1 %collective-permute-start.1 = (bf16[2,2,128,128]{3,2,1,0:T(8,128)(2,1)S(1)}, bf16[2,2,128,128]{3,2,1,0:T(8,128)(2,1)S(1)}, u32[]{:S(2)}, u32[]{:S(2)}) collective-permute-start(bf16[2,2,128,128]{3,2,1,0:T(8,128)(2,1)S(1)} %pad_maximum_fusion.1), channel_id=1, source_target_pairs={{0,8},{4,12},{8,0},{12,4},{16,24},{20,28},{24,16},{28,20},{1,9},{5... | collective-permute-start | bytes 393224 | tf_op jit(solution)/shard_map/ppermute | solution.py:25
  17.6 0.1 convert_reduce_fusion.1
  17.7 2.8 %collective-permute-done.1 = bf16[2,2,128,128]{3,2,1,0:T(8,128)(2,1)S(1)} collective-permute-done((bf16[2,2,128,128]{3,2,1,0:T(8,128)(2,1)S(1)}, bf16[2,2,128,128]{3,2,1,0:T(8,128)(2,1)S(1)}, u32[]{:S(2)}, u32[]{:S(2)}) %collective-permute-start.1) | collective-permute-done | bytes 131104 | tf_op jit(solution)/shard_map/ppermute | solution.py:25
  20.6 3.1 %collective-permute-start.2 = (bf16[4,2,128,128]{3,2,1,0:T(8,128)(2,1)S(1)}, bf16[4,2,128,128]{3,2,1,0:T(8,128)(2,1)S(1)}, u32[]{:S(2)}, u32[]{:S(2)}) collective-permute-start(bf16[4,2,128,128]{3,2,1,0:T(8,128)(2,1)S(1)} %pad_maximum_fusion), channel_id=1, source_target_pairs={{0,16},{4,20},{8,24},{12,28},{16,0},{20,4},{24,8},{28,12},{1,17},{... | collective-permute-start | bytes 786440 | tf_op jit(solution)/shard_map/ppermute | solution.py:25
  23.7 1.1 %copy.15 = bf16[128,896]{0,1:T(8,128)(2,1)S(1)} copy(bf16[128,896]{1,0:T(8,128)(2,1)} %param.8) | data formatting | bytes 458752 | tf_op args[0]
  24.8 0.8 dynamic_slice.3
  25.6 0.0 copy-done
  25.6 0.1 broadcast.312
  25.6 2.8 %gather_fusion = s32[1024,128]{1,0:T(8,128)S(1)} fusion(s32[128,8]{0,1:T(8,128)S(1)} %broadcast.312, s32[1024]{0:T(1024)S(1)} %broadcast_clamp_fusion), kind=kCustom, calls=%fused_computation | custom fusion | bytes 1052672 | tf_op jit(solution)/shard_map/jit(_take)/gather | solution.py:70
  28.4 0.0 copy-done.2
  28.4 1.0 %fusion.16 = pred[128,1024]{0,1:T(8,128)(4,1)S(1)} fusion(s32[1024,128]{1,0:T(8,128)S(1)} %gather_fusion, s32[128]{0:T(128)S(1)} %get-tuple-element.19, s32[128]{0:T(128)S(1)} %dynamic_slice.3, s32[128]{0:T(128)S(1)} %convert_reduce_fusion.1, s32[128]{0:T(128)S(1)} %get-tuple-element.20, s32[1024]{0:T(1024)S(1)} %add_select_fusion, s32[1024]{0:T(1024)S(1)} %copy-done.2, ...), kind=kLoop, calls=%fused_computation.16 | loop fusion | flops 1310720 | bytes 670720 | tf_op jit(solution)/shard_map/and | solution.py:73
  29.5 3.8 %collective-permute-done.2 = bf16[4,2,128,128]{3,2,1,0:T(8,128)(2,1)S(1)} collective-permute-done((bf16[4,2,128,128]{3,2,1,0:T(8,128)(2,1)S(1)}, bf16[4,2,128,128]{3,2,1,0:T(8,128)(2,1)S(1)}, u32[]{:S(2)}, u32[]{:S(2)}) %collective-permute-start.2) | collective-permute-done | bytes 262176 | tf_op jit(solution)/shard_map/ppermute | solution.py:25
  33.4 0.7 fusion.1
  34.1 0.0 copy-start.1
  34.2 1.8 %copy-done.1 = f32[1024,128,7]{1,0,2:T(8,128)} copy-done((f32[1024,128,7]{1,0,2:T(8,128)}, f32[1024,128,7]{1,0,2:T(8,128)S(1)}, u32[]{:S(2)}) %copy-start.1) | copy-done | bytes 3670040
  35.9 0.9 %fusion.2 = f32[7,128]{1,0:T(8,128)S(1)} fusion(f32[1024,128,7]{1,0,2:T(8,128)S(1)} %get-tuple-element.16, f32[7,128]{1,0:T(8,128)S(1)} %broadcast_maximum_fusion, pred[128,1024]{0,1:T(8,128)(4,1)S(1)} %fusion.16), kind=kLoop, calls=%fused_computation.6 | loop fusion | flops 4586624 | bytes 3808256 | tf_op jit(solution)/shard_map/reduce_sum | solution.py:85
  36.8 6.5 %fusion = bf16[128,3584]{1,0:T(8,128)(2,1)S(1)} fusion(bf16[7,128,3584]{2,1,0:T(8,128)(2,1)} %bitcast.70, bf16[1024,128,1]{1,0,2:T(8,128)(2,1)S(1)} %bitcast.65, f32[1024,128,7]{1,0,2:T(8,128)} %copy-done.1, f32[7,128]{1,0:T(8,128)S(1)} %broadcast_maximum_fusion, pred[128,1024]{0,1:T(8,128)(4,1)S(1)} %fusion.16, f32[7,128]{1,0:T(8,128)S(1)} %fusion.2), kind=kOutput, calls=%fused_computation.2 | convolution fusion | flops 1062240256 | bytes 11410432 | tf_op jit(solution)/shard_map/gqd,gde->qe/dot_general | solution.py:93
  43.3 1.3 %copy.20 = bf16[128,3584]{0,1:T(8,128)(2,1)} copy(bf16[128,3584]{1,0:T(8,128)(2,1)S(1)} %fusion) | data formatting | bytes 1835008
  44.6 0.0 reduce-scatter.4.cloned.1.call-update
  44.6 25.3 %reduce-scatter.4.cloned.1.call-done = bf16[896,128]{1,0:T(8,128)(2,1)} async-done(((bf16[3584,128]{1,0:T(8,128)(2,1)}), bf16[896,128]{1,0:T(8,128)(2,1)}) %reduce-scatter.4.cloned.1.call-update) | async-done | bytes 229392
  70.0 1.8 %copy.21 = bf16[128,896]{1,0:T(8,128)(2,1)} copy(bf16[128,896]{0,1:T(8,128)(2,1)} %bitcast.66) | data formatting | bytes 458752
  (14 shorter events, 0.2 us)
Async XLA Ops:
  6.5 19.0 %copy-start = (s32[1,8]{1,0:T(1,128)S(1)}, s32[1,8]{1,0:T(1,128)}, u32[]{:S(2)}) copy-start(s32[1,8]{1,0:T(1,128)} %param.14) | copy-start | bytes 100
  6.5 21.9 %copy-start.2 = (s32[1024]{0:T(1024)S(1)}, s32[1024]{0:T(1024)}, u32[]{:S(2)}) copy-start(s32[1024]{0:T(1024)} %param.13) | copy-start | bytes 12292
  6.5 63.4 %reduce-scatter.4.cloned.1.call-start = ((), (), s32[]{:S(2)}) async-start(), calls=%async_computation.1 | async-start | bytes 1146880
  10.1 5.3 %collective-permute-start = (bf16[1,2,128,128]{3,2,1,0:T(8,128)(2,1)S(1)}, bf16[1,2,128,128]{3,2,1,0:T(8,128)(2,1)S(1)}, u32[]{:S(2)}, u32[]{:S(2)}) collective-permute-start(bf16[1,2,128,128]{3,2,1,0:T(8,128)(2,1)S(1)} %maximum_bitcast_fusion.1), channel_id=1, source_target_pairs={{0,4},{4,0},{8,12},{12,8},{16,20},{20,16},{24,28},{28,24},{1,5},{5... | collective-permute-start | bytes 196616 | tf_op jit(solution)/shard_map/ppermute | solution.py:25
  15.4 5.1 %collective-permute-start.1 = (bf16[2,2,128,128]{3,2,1,0:T(8,128)(2,1)S(1)}, bf16[2,2,128,128]{3,2,1,0:T(8,128)(2,1)S(1)}, u32[]{:S(2)}, u32[]{:S(2)}) collective-permute-start(bf16[2,2,128,128]{3,2,1,0:T(8,128)(2,1)S(1)} %pad_maximum_fusion.1), channel_id=1, source_target_pairs={{0,8},{4,12},{8,0},{12,4},{16,24},{20,28},{24,16},{28,20},{1,9},{5... | collective-permute-start | bytes 393224 | tf_op jit(solution)/shard_map/ppermute | solution.py:25
  20.6 12.7 %collective-permute-start.2 = (bf16[4,2,128,128]{3,2,1,0:T(8,128)(2,1)S(1)}, bf16[4,2,128,128]{3,2,1,0:T(8,128)(2,1)S(1)}, u32[]{:S(2)}, u32[]{:S(2)}) collective-permute-start(bf16[4,2,128,128]{3,2,1,0:T(8,128)(2,1)S(1)} %pad_maximum_fusion), channel_id=1, source_target_pairs={{0,16},{4,20},{8,24},{12,28},{16,0},{20,4},{24,8},{28,12},{1,17},{... | collective-permute-start | bytes 786440 | tf_op jit(solution)/shard_map/ppermute | solution.py:25
  34.1 1.8 %copy-start.1 = (f32[1024,128,7]{1,0,2:T(8,128)}, f32[1024,128,7]{1,0,2:T(8,128)S(1)}, u32[]{:S(2)}) copy-start(f32[1024,128,7]{1,0,2:T(8,128)S(1)} %get-tuple-element.16) | copy-start | bytes 11010052
Sparse Core Ops, SparseCore 0:
  44.8 25.1 reduce-scatter.3
